TPU v7x, 512 devices: a whole 4x8x8 slice. The times are simulated.
512 devices in a mesh: gx: 16 (over y_hi, x, core), gy: 4 (over y_lo), gz: 8 (over z).
Axes of the slice: x: 4, y: 8 (y_hi: 2, y_lo: 4; y = y_hi * 4 + y_lo), z: 8, core: 2. Of those that a mesh axis runs over, the one named last changes fastest.
Arguments:
- velocity: float32 [3, 32, 4, 32, 512], P(None, 'gx', 'gy', 'gz'), may hold values from -4 to 4
- reaction: float32 [32, 4, 32, 512], P('gx', 'gy', 'gz'), may hold values from 10 to 100
Outputs:
- velocity_out: float32 [3, 32, 4, 32, 512], P(None, 'gx', 'gy', 'gz')
- pressure: float32 [32, 4, 32, 512], P('gx', 'gy', 'gz')
- residual: float32 [32, 4, 32, 512], P('gx', 'gy', 'gz')
All inputs are finite; a program needn't handle non-finite values.
Results may differ from a plain program's by a relative error of at most 0.007.
Values sent between devices are 32-bit elements; how exact they have to be, the bound alone decides.
A program may use at most 64 MiB of HBM per device.

v0:
```python
import jax
import jax.numpy as jnp
import numpy as np
from jax import lax
from jax.sharding import PartitionSpec as P

SUBSTEPS = 2
ITERS = 4
step_size = 0.02


def extended(block, sides, width, periodic):
    for axis, dim in sides:
        count = lax.axis_size(axis)
        forward = [(i, i + 1) for i in range(count - 1)]
        if periodic:
            forward.append((count - 1, 0))
        backward = [(target, source) for source, target in forward]
        low = lax.ppermute(
            lax.slice_in_dim(block, block.shape[dim] - width, None, axis=dim), axis, forward
        )
        high = lax.ppermute(lax.slice_in_dim(block, 0, width, axis=dim), axis, backward)
        block = jnp.concatenate([low, block, high], axis=dim)
    return block


def legendre_seven(points):
    earlier = points * 0.0 + 1.0
    current = points
    for degree in range(1, 7):
        earlier, current = (
            current,
            ((2 * degree + 1) * points * current - degree * earlier) / (degree + 1),
        )
    return current


def tables():
    half = np.array([0.20929921790247888, 0.5917001814331423, 0.8717401485096066, 1.0])
    points = np.concatenate([-half[::-1], half])
    legendre = legendre_seven(points)
    weights = 2.0 / (56.0 * legendre**2)
    spacing = points[:, None] - points[None, :] + np.eye(8)
    derivative = legendre[:, None] / legendre[None, :] / spacing * (1.0 - np.eye(8))
    derivative[0, 0] = -14.0
    derivative[7, 7] = 14.0
    return (jnp.asarray(weights, jnp.float32), jnp.asarray(derivative, jnp.float32))


def derive(values, derivative, along_dim, transposed):
    layout = values.shape
    matrix = derivative.T if transposed else derivative
    blocks = values.reshape(-1, 8, 8, 8)
    patterns = ("aq,nqbc->nabc", "bq,naqc->nabc", "cq,nabq->nabc")
    result = jnp.einsum(patterns[along_dim], matrix, blocks, precision=lax.Precision.HIGHEST)
    return result.reshape(layout)


def place_face(values, target_axis, position, update):
    selector = tuple(
        (position if place == target_axis else slice(None) for place in range(values.ndim))
    )
    return values.at[selector].set(update)


def faces_along_x(sequence):
    return extended(sequence, (("gx", 0),), 1, True)


def faces_along_y(sequence):
    return extended(sequence, (("gy", 0),), 1, False)


def faces_along_z(sequence):
    return extended(sequence, (("gz", 0),), 1, False)


def join_faces(values, along_dim, exchanger):
    lower_face = jnp.moveaxis(jnp.take(values, 0, axis=4 + along_dim), 1 + along_dim, 0)
    upper_face = jnp.moveaxis(jnp.take(values, 7, axis=4 + along_dim), 1 + along_dim, 0)
    elements = lower_face.shape[0]
    face_shape = lower_face.shape
    sequence = jnp.stack([lower_face, upper_face], axis=1).reshape(2 * elements, -1)
    padded = exchanger(sequence)
    paired = padded.reshape(elements + 1, 2, -1)
    totals = paired[:, 0] + paired[:, 1]
    new_lower = jnp.moveaxis(totals[:-1].reshape(face_shape), 0, 1 + along_dim)
    new_upper = jnp.moveaxis(totals[1:].reshape(face_shape), 0, 1 + along_dim)
    values = place_face(values, 4 + along_dim, 0, new_lower)
    return place_face(values, 4 + along_dim, 7, new_upper)


def assemble(values):
    exchangers = (faces_along_x, faces_along_y, faces_along_z)
    dim_order = (0, 1, 2)
    for along_dim in dim_order:
        values = join_faces(values, along_dim, exchangers[along_dim])
    return values


def dim_factors(local_count, offset, total_count, bounded_by_walls):
    element_ids = offset + jnp.arange(local_count)
    node_ids = jnp.arange(8)
    at_end = (node_ids[None, :] == 0) | (node_ids[None, :] == 7)
    low_wall = (element_ids[:, None] == 0) & (node_ids[None, :] == 0)
    high_wall = (element_ids[:, None] == total_count - 1) & (node_ids[None, :] == 7)
    on_wall = (low_wall | high_wall) & bounded_by_walls
    shared = at_end & jnp.logical_not(on_wall)
    return (jnp.where(shared, 2.0, 1.0).astype(jnp.float32), on_wall.astype(jnp.float32))


def body(velocity, reaction):
    weights, derivative = tables()
    count_x, count_y, count_z = (reaction.shape[0], reaction.shape[1], reaction.shape[2])
    speed = velocity.reshape(3, count_x, count_y, count_z, 8, 8, 8)
    react = reaction.reshape(1, count_x, count_y, count_z, 8, 8, 8)
    mass_matrix = weights[:, None, None] * weights[None, :, None] * weights[None, None, :]
    factor_x, wall_x = dim_factors(
        count_x, lax.axis_index("gx") * count_x, lax.axis_size("gx") * count_x, False
    )
    factor_y, wall_y = dim_factors(
        count_y, lax.axis_index("gy") * count_y, lax.axis_size("gy") * count_y, True
    )
    factor_z, wall_z = dim_factors(
        count_z, lax.axis_index("gz") * count_z, lax.axis_size("gz") * count_z, True
    )
    multiplicity = (
        factor_x[None, :, None, None, :, None, None]
        * factor_y[None, None, :, None, None, :, None]
        * factor_z[None, None, None, :, None, None, :]
    )
    interior = (1.0 - wall_y[None, None, :, None, None, :, None]) * (
        1.0 - wall_z[None, None, None, :, None, None, :]
    )
    stiff_sum = jnp.sum(weights[:, None] * derivative * derivative, axis=0)
    diag_local = (
        stiff_sum[:, None, None] * weights[None, :, None] * weights[None, None, :]
        + weights[:, None, None] * stiff_sum[None, :, None] * weights[None, None, :]
        + weights[:, None, None] * weights[None, :, None] * stiff_sum[None, None, :]
    )
    diag_terms = diag_local + react * mass_matrix
    speed = assemble(speed) / multiplicity
    diagonal = None
    for substep in range(SUBSTEPS):
        gradient_fields = [derive(speed, derivative, along_dim, False) for along_dim in range(3)]
        transport = (
            speed[0:1] * gradient_fields[0]
            + speed[1:2] * gradient_fields[1]
            + speed[2:3] * gradient_fields[2]
        )
        tendency = assemble(mass_matrix * transport) / (mass_matrix * multiplicity)
        speed = interior * (speed - step_size * tendency)
    spread = (
        derive(speed[0:1], derivative, 0, False)
        + derive(speed[1:2], derivative, 1, False)
        + derive(speed[2:3], derivative, 2, False)
    )
    source = -assemble(mass_matrix * spread)
    diagonal = assemble(diag_terms)

    def local_inner(first, second):
        return jnp.sum(first * second / multiplicity)

    def norm_weighted_mass(residual_vec, precond_vec):
        return lax.psum(local_inner(residual_vec, precond_vec), ("gx", "gy", "gz"))

    pressure = jnp.zeros_like(source)
    residual = source
    precond = residual / diagonal
    search = precond
    progress = norm_weighted_mass(residual, precond)
    for sweep_index in range(ITERS):
        local_sum = react * mass_matrix * search
        for apply_along_dim in range(3):
            local_sum = local_sum + derive(
                mass_matrix * derive(search, derivative, apply_along_dim, False),
                derivative,
                apply_along_dim,
                True,
            )
        applied = assemble(local_sum)
        step_length = progress / lax.psum(local_inner(search, applied), ("gx", "gy", "gz"))
        pressure = pressure + step_length * search
        residual = residual - step_length * applied
        precond = residual / diagonal
        progress_next = norm_weighted_mass(residual, precond)
        search = precond + progress_next / progress * search
        progress = progress_next
    return (
        speed.reshape(3, count_x, count_y, count_z, 512),
        pressure.reshape(count_x, count_y, count_z, 512),
        residual.reshape(count_x, count_y, count_z, 512),
    )


def solution(mesh):
    in_specs = (P(None, "gx", "gy", "gz", None), P("gx", "gy", "gz", None))
    out_specs = (
        P(None, "gx", "gy", "gz", None),
        P("gx", "gy", "gz", None),
        P("gx", "gy", "gz", None),
    )
    return jax.shard_map(body, mesh=mesh, in_specs=in_specs, out_specs=out_specs, check_vma=False)
```

profile of v0, /device:TPU:1, one launch (start us, length us, event | category | flops | bytes accessed | tf_op | source)
XLA Modules:
  0.0 1127.1 jit_solution(3727668878768256225)
XLA Ops:
  6.6 6.2 collective-permute-start.1
  15.8 9.7 collective-permute-start.25
  54.8 15.4 %scatter.189 = f32[3,2,1,4,8,8,8]{6,5,4,3,1,0,2:T(8,128)S(1)} dynamic-update-slice(f32[3,2,1,4,8,8,8]{6,5,4,3,1,0,2:T(8,128)S(1)} %scatter.186, f32[3,2,1,4,8,8,1]{6,5,4,3,1,0,2:T(8,128)S(1)} %copy.186, s32[]{:T(128)} %constant.1319.clone.1, s32[]{:T(128)} %constant.1319.clone.1, s32[]{:T(128)} %constant.1319.clone.1, s32[]{:T(128)} %constant.1319.clone.1, s32[]{:T(128)} %constant.1319.clone.1, ...) | dynamic-update-slice | bytes 12292 | tf_op jit(solution)/shard_map/scatter | solution.py:63
  81.6 12.9 %collective-permute-start.7 = (f32[1,768]{1,0:T(1,128)S(1)}, f32[1,768]{1,0:T(1,128)S(1)}, u32[]{:S(2)}, u32[]{:S(2)}) collective-permute-start(f32[1,768]{1,0:T(1,128)S(1)} %get-tuple-element.938), channel_id=1, source_target_pairs={{32,0},{64,32},{96,64},{128,96},{160,128},{192,160},{224,192},{256... | collective-permute-start | bytes 9224 | tf_op jit(solution)/shard_map/ppermute | solution.py:22
  114.5 4.7 collective-permute-done.11
  127.5 15.4 %scatter.199 = f32[3,2,1,4,8,8,8]{6,5,4,3,1,0,2:T(8,128)S(1)} dynamic-update-slice(f32[3,2,1,4,8,8,8]{6,5,4,3,1,0,2:T(8,128)S(1)} %scatter.196, f32[3,2,1,4,8,8,1]{6,5,4,3,1,0,2:T(8,128)S(1)} %copy.203, s32[]{:T(128)} %constant.1319.clone.1, s32[]{:T(128)} %constant.1319.clone.1, s32[]{:T(128)} %constant.1319.clone.1, s32[]{:T(128)} %constant.1319.clone.1, s32[]{:T(128)} %constant.1319.clone.1, ...) | dynamic-update-slice | bytes 12292 | tf_op jit(solution)/shard_map/scatter | solution.py:63
  152.4 12.7 %collective-permute-start.13 = (f32[1,768]{1,0:T(1,128)S(1)}, f32[1,768]{1,0:T(1,128)S(1)}, u32[]{:S(2)}, u32[]{:S(2)}) collective-permute-start(f32[1,768]{1,0:T(1,128)S(1)} %get-tuple-element.930), channel_id=1, source_target_pairs={{32,0},{64,32},{96,64},{128,96},{160,128},{192,160},{224,192},{256... | collective-permute-start | bytes 9224 | tf_op jit(solution)/shard_map/ppermute | solution.py:22
  165.2 4.8 collective-permute-start.28
  199.0 15.4 %scatter.209 = f32[3,2,1,4,8,8,8]{6,5,4,3,1,0,2:T(8,128)S(1)} dynamic-update-slice(f32[3,2,1,4,8,8,8]{6,5,4,3,1,0,2:T(8,128)S(1)} %scatter.206, f32[3,2,1,4,8,8,1]{6,5,4,3,1,0,2:T(8,128)S(1)} %copy.220, s32[]{:T(128)} %constant.1319.clone.1, s32[]{:T(128)} %constant.1319.clone.1, s32[]{:T(128)} %constant.1319.clone.1, s32[]{:T(128)} %constant.1319.clone.1, s32[]{:T(128)} %constant.1319.clone.1, ...) | dynamic-update-slice | bytes 12292 | tf_op jit(solution)/shard_map/scatter | solution.py:63
  219.2 12.8 %collective-permute-start.19 = (f32[1,256]{1,0:T(1,128)S(1)}, f32[1,256]{1,0:T(1,128)S(1)}, u32[]{:S(2)}, u32[]{:S(2)}) collective-permute-start(f32[1,256]{1,0:T(1,128)S(1)} %get-tuple-element.992), channel_id=1, source_target_pairs={{32,0},{64,32},{96,64},{128,96},{160,128},{192,160},{224,192},{256... | collective-permute-start | bytes 3080 | tf_op jit(solution)/shard_map/ppermute | solution.py:22
  246.7 4.6 scatter.229
  252.8 4.8 scatter.219
  263.0 11.8 %collective-permute-start.31 = (f32[1,256]{1,0:T(1,128)S(1)}, f32[1,256]{1,0:T(1,128)S(1)}, u32[]{:S(2)}, u32[]{:S(2)}) collective-permute-start(f32[1,256]{1,0:T(1,128)S(1)} %get-tuple-element.986), channel_id=1, source_target_pairs={{32,0},{64,32},{96,64},{128,96},{160,128},{192,160},{224,192},{256... | collective-permute-start | bytes 3080 | tf_op jit(solution)/shard_map/ppermute | solution.py:22
  293.7 4.6 scatter.239
  299.1 107.2 %all-reduce = (f32[]{:T(128)}, f32[]{:T(128)}) all-reduce(f32[]{:T(128)} %get-tuple-element.811, f32[]{:T(128)} %get-tuple-element.810), channel_id=1, replica_groups=mesh['gx'=16,'gy'=4,'gz'=8] {'gx','gy','gz'}, use_global_device_ids=true, to_apply=%region_2.15 | all-reduce | flops 2 | bytes 16 | tf_op jit(solution)/shard_map/psum | solution.py:165
  408.4 94.4 %psum.58 = f32[]{:T(128)} all-reduce(f32[]{:T(128)} %get-tuple-element.862), channel_id=1, replica_groups=mesh['gx'=16,'gy'=4,'gz'=8] {'gx','gy','gz'}, use_global_device_ids=true, to_apply=%region_6.19 | all-reduce | flops 1 | bytes 8 | tf_op jit(solution)/shard_map/psum | solution.py:165
  535.5 4.6 scatter.249
  540.9 104.3 %psum.59 = f32[]{:T(128)} all-reduce(f32[]{:T(128)} %fusion.31), channel_id=1, replica_groups=mesh['gx'=16,'gy'=4,'gz'=8] {'gx','gy','gz'}, use_global_device_ids=true, to_apply=%region_8.21 | all-reduce | flops 1 | bytes 8 | tf_op jit(solution)/shard_map/psum | solution.py:182
  647.9 94.4 %psum.60 = f32[]{:T(128)} all-reduce(f32[]{:T(128)} %get-tuple-element.859), channel_id=1, replica_groups=mesh['gx'=16,'gy'=4,'gz'=8] {'gx','gy','gz'}, use_global_device_ids=true, to_apply=%region_10.23 | all-reduce | flops 1 | bytes 8 | tf_op jit(solution)/shard_map/psum | solution.py:165
  774.1 4.6 scatter.259
  779.5 103.8 %psum.61 = f32[]{:T(128)} all-reduce(f32[]{:T(128)} %fusion.33), channel_id=1, replica_groups=mesh['gx'=16,'gy'=4,'gz'=8] {'gx','gy','gz'}, use_global_device_ids=true, to_apply=%region_12.25 | all-reduce | flops 1 | bytes 8 | tf_op jit(solution)/shard_map/psum | solution.py:182
  886.0 94.7 %psum.62 = f32[]{:T(128)} all-reduce(f32[]{:T(128)} %get-tuple-element.856), channel_id=1, replica_groups=mesh['gx'=16,'gy'=4,'gz'=8] {'gx','gy','gz'}, use_global_device_ids=true, to_apply=%region_14.27 | all-reduce | flops 1 | bytes 8 | tf_op jit(solution)/shard_map/psum | solution.py:165
  1012.5 4.6 scatter.269
  1018.9 103.9 %psum.63 = f32[]{:T(128)} all-reduce(f32[]{:T(128)} %fusion.35), channel_id=1, replica_groups=mesh['gx'=16,'gy'=4,'gz'=8] {'gx','gy','gz'}, use_global_device_ids=true, to_apply=%region_16.29 | all-reduce | flops 1 | bytes 8 | tf_op jit(solution)/shard_map/psum | solution.py:182
  (571 shorter events, 260.7 us)
Async XLA Ops:
  2.1 27.2 %collective-permute-start = (f32[1,768]{1,0:T(1,128)S(1)}, f32[1,768]{1,0:T(1,128)S(1)}, u32[]{:S(2)}, u32[]{:S(2)}) collective-permute-start(f32[1,768]{1,0:T(1,128)S(1)} %get-tuple-element.945), channel_id=1, source_target_pairs={{0,32},{32,64},{64,96},{96,128},{128,160},{160,192},{192,224},{224... | collective-permute-start | bytes 9224 | tf_op jit(solution)/shard_map/ppermute | solution.py:19
  6.6 22.7 %collective-permute-start.1 = (f32[1,768]{1,0:T(1,128)S(1)}, f32[1,768]{1,0:T(1,128)S(1)}, u32[]{:S(2)}, u32[]{:S(2)}) collective-permute-start(f32[1,768]{1,0:T(1,128)S(1)} %get-tuple-element.946), channel_id=1, source_target_pairs={{32,0},{64,32},{96,64},{128,96},{160,128},{192,160},{224,192},{256... | collective-permute-start | bytes 9224 | tf_op jit(solution)/shard_map/ppermute | solution.py:22
  13.9 12.1 %collective-permute-start.24 = (f32[1,256]{1,0:T(1,128)S(1)}, f32[1,256]{1,0:T(1,128)S(1)}, u32[]{:S(2)}, u32[]{:S(2)}) collective-permute-start(f32[1,256]{1,0:T(1,128)S(1)} %get-tuple-element.997), channel_id=1, source_target_pairs={{0,32},{32,64},{64,96},{96,128},{128,160},{160,192},{192,224},{224... | collective-permute-start | bytes 3080 | tf_op jit(solution)/shard_map/ppermute | solution.py:19
  15.8 10.5 collective-permute-start.25
  26.7 8.7 collective-permute-start.26
  28.1 7.3 collective-permute-start.27
  79.4 15.9 %collective-permute-start.6 = (f32[1,768]{1,0:T(1,128)S(1)}, f32[1,768]{1,0:T(1,128)S(1)}, u32[]{:S(2)}, u32[]{:S(2)}) collective-permute-start(f32[1,768]{1,0:T(1,128)S(1)} %get-tuple-element.937), channel_id=1, source_target_pairs={{0,32},{32,64},{64,96},{96,128},{128,160},{160,192},{192,224},{224... | collective-permute-start | bytes 9224 | tf_op jit(solution)/shard_map/ppermute | solution.py:19
  81.6 13.7 %collective-permute-start.7 = (f32[1,768]{1,0:T(1,128)S(1)}, f32[1,768]{1,0:T(1,128)S(1)}, u32[]{:S(2)}, u32[]{:S(2)}) collective-permute-start(f32[1,768]{1,0:T(1,128)S(1)} %get-tuple-element.938), channel_id=1, source_target_pairs={{32,0},{64,32},{96,64},{128,96},{160,128},{192,160},{224,192},{256... | collective-permute-start | bytes 9224 | tf_op jit(solution)/shard_map/ppermute | solution.py:22
  113.1 6.2 collective-permute-start.11
  150.5 20.8 %collective-permute-start.12 = (f32[1,768]{1,0:T(1,128)S(1)}, f32[1,768]{1,0:T(1,128)S(1)}, u32[]{:S(2)}, u32[]{:S(2)}) collective-permute-start(f32[1,768]{1,0:T(1,128)S(1)} %get-tuple-element.929), channel_id=1, source_target_pairs={{0,32},{32,64},{64,96},{96,128},{128,160},{160,192},{192,224},{224... | collective-permute-start | bytes 9224 | tf_op jit(solution)/shard_map/ppermute | solution.py:19
  152.4 18.9 %collective-permute-start.13 = (f32[1,768]{1,0:T(1,128)S(1)}, f32[1,768]{1,0:T(1,128)S(1)}, u32[]{:S(2)}, u32[]{:S(2)}) collective-permute-start(f32[1,768]{1,0:T(1,128)S(1)} %get-tuple-element.930), channel_id=1, source_target_pairs={{32,0},{64,32},{96,64},{128,96},{160,128},{192,160},{224,192},{256... | collective-permute-start | bytes 9224 | tf_op jit(solution)/shard_map/ppermute | solution.py:22
  165.2 11.8 %collective-permute-start.28 = (f32[1,128]{1,0:T(1,128)S(1)}, f32[1,128]{1,0:T(1,128)S(1)}, u32[]{:S(2)}, u32[]{:S(2)}) collective-permute-start(f32[1,128]{1,0:T(1,128)S(1)} %get-tuple-element.995), channel_id=1, source_target_pairs={{0,1},{1,2},{2,3},{3,4},{4,5},{5,6},{6,7},{8,9},{9,10},{10,11},{11... | collective-permute-start | bytes 1544 | tf_op jit(solution)/shard_map/ppermute | solution.py:19
  170.0 7.0 collective-permute-start.29
  185.1 5.6 collective-permute-start.16
  217.2 14.7 %collective-permute-start.18 = (f32[1,256]{1,0:T(1,128)S(1)}, f32[1,256]{1,0:T(1,128)S(1)}, u32[]{:S(2)}, u32[]{:S(2)}) collective-permute-start(f32[1,256]{1,0:T(1,128)S(1)} %get-tuple-element.991), channel_id=1, source_target_pairs={{0,32},{32,64},{64,96},{96,128},{128,160},{160,192},{192,224},{224... | collective-permute-start | bytes 3080 | tf_op jit(solution)/shard_map/ppermute | solution.py:19
  219.2 13.6 %collective-permute-start.19 = (f32[1,256]{1,0:T(1,128)S(1)}, f32[1,256]{1,0:T(1,128)S(1)}, u32[]{:S(2)}, u32[]{:S(2)}) collective-permute-start(f32[1,256]{1,0:T(1,128)S(1)} %get-tuple-element.992), channel_id=1, source_target_pairs={{32,0},{64,32},{96,64},{128,96},{160,128},{192,160},{224,192},{256... | collective-permute-start | bytes 3080 | tf_op jit(solution)/shard_map/ppermute | solution.py:22
  240.3 11.0 collective-permute-start.22
  243.9 7.4 collective-permute-start.23
  261.1 13.8 %collective-permute-start.30 = (f32[1,256]{1,0:T(1,128)S(1)}, f32[1,256]{1,0:T(1,128)S(1)}, u32[]{:S(2)}, u32[]{:S(2)}) collective-permute-start(f32[1,256]{1,0:T(1,128)S(1)} %get-tuple-element.985), channel_id=1, source_target_pairs={{0,32},{32,64},{64,96},{96,128},{128,160},{160,192},{192,224},{224... | collective-permute-start | bytes 3080 | tf_op jit(solution)/shard_map/ppermute | solution.py:19
  263.0 12.7 %collective-permute-start.31 = (f32[1,256]{1,0:T(1,128)S(1)}, f32[1,256]{1,0:T(1,128)S(1)}, u32[]{:S(2)}, u32[]{:S(2)}) collective-permute-start(f32[1,256]{1,0:T(1,128)S(1)} %get-tuple-element.986), channel_id=1, source_target_pairs={{32,0},{64,32},{96,64},{128,96},{160,128},{192,160},{224,192},{256... | collective-permute-start | bytes 3080 | tf_op jit(solution)/shard_map/ppermute | solution.py:22
  283.2 5.6 collective-permute-start.34
  507.7 6.2 collective-permute-start.36
  747.1 6.2 collective-permute-start.42
  985.5 6.2 collective-permute-start.48
  (38 other events, 253.8 us)
where the time goes:
time: 1140 us; the launch traced here: 1130 us
  blocking collectives  703 us (62%)
  starting transfers between devices  176 us (15%)
  local copies, waits for them, and re-layouts  148 us (13%)
  waiting for transfers between devices  60.7 us (5%)
  matrix products  17.8 us (2%)
  between operations  13.6 us (1%)
    psum x4, blocking collectives, norm_weighted_mass(): return lax.psum(local_inner(residual_vec, precond_vec), ('gx', 'gy', 'gz'))  391 us
    psum x3, blocking collectives, body(): lax.psum(local_inner(search, applied), ('gx', 'gy', 'gz'))  312 us
    scatter x54, local copies, waits for them, and re-layouts, place_face(): return values.at[selector].set(update)  98.6 us
    ppermute x27, starting transfers between devices, extended(): lax.ppermute(lax.slice_in_dim(block, 0, width, axis=dim), axis, backward)  95.5 us
    ppermute x27, starting transfers between devices, extended(): lax.ppermute(lax.slice_in_dim(block, block.shape[dim] - width, None, axis...  80.1 us
    ppermute x27, waiting for transfers between devices, extended(): lax.ppermute(lax.slice_in_dim(block, 0, width, axis=dim), axis, backward)  60.7 us
  transfers between devices with their start and end apart: 54, of which 21 were waited for; matrix products, arithmetic and copies ran while one was open for 1% of the time, Pallas kernels for 0%

commit v1 on v0

--- a/solution.py
+++ b/solution.py
@@ -3,6 +3,7 @@
 import numpy as np
 from jax import lax
 from jax.sharding import PartitionSpec as P
+from jax.lax import psum
 
 SUBSTEPS = 2
 ITERS = 4
@@ -179,7 +180,12 @@
                 True,
             )
         applied = assemble(local_sum)
-        step_length = progress / lax.psum(local_inner(search, applied), ("gx", "gy", "gz"))
+
+        def point_the_meshes(block_in):
+            a_now = psum(psum(block_in, ("gy", "gz")), "gx")
+            return a_now
+
+        step_length = progress / point_the_meshes(local_inner(search, applied))
         pressure = pressure + step_length * search
         residual = residual - step_length * applied
         precond = residual / diagonal

time: 1140 us -> 1310 us (1.15)
  blocking collectives: 703 us -> 883 us
    psum x3 -> x8, blocking collectives: 312 us -> 508 us  [point_the_meshes(): a_now = psum(psum(block_in, ('gy', 'gz')), 'gx')]
    psum x4, blocking collectives: 391 us -> 375 us  [norm_weighted_mass(): return lax.psum(local_inner(residual_vec, precond_vec), ('gx', 'gy', 'gz'))]
where the time goes in v1:
time: 1310 us; the launch traced here: 1300 us
  blocking collectives  883 us (67%)
  starting transfers between devices  173 us (13%)
  local copies, waits for them, and re-layouts  148 us (11%)
  waiting for transfers between devices  58 us (4%)
  matrix products  17.9 us (1%)
  between operations  13.6 us (1%)
    psum x8, blocking collectives, point_the_meshes(): a_now = psum(psum(block_in, ('gy', 'gz')), 'gx')  508 us
    psum x4, blocking collectives, norm_weighted_mass(): return lax.psum(local_inner(residual_vec, precond_vec), ('gx', 'gy', 'gz'))  375 us
    scatter x54, local copies, waits for them, and re-layouts, place_face(): return values.at[selector].set(update)  98.5 us
    ppermute x27, starting transfers between devices, extended(): lax.ppermute(lax.slice_in_dim(block, 0, width, axis=dim), axis, backward)  95.7 us
    ppermute x27, starting transfers between devices, extended(): lax.ppermute(lax.slice_in_dim(block, block.shape[dim] - width, None, axis...  77.4 us
    ppermute x27, waiting for transfers between devices, extended(): lax.ppermute(lax.slice_in_dim(block, 0, width, axis=dim), axis, backward)  57.9 us
  transfers between devices with their start and end apart: 54, of which 21 were waited for; matrix products, arithmetic and copies ran while one was open for 1% of the time, Pallas kernels for 0%

profile of v1, /device:TPU:1, one launch (start us, length us, event | category | flops | bytes accessed | tf_op | source)
XLA Modules:
  0.0 1302.4 jit_solution(16557383342931311009)
XLA Ops:
  6.6 6.2 collective-permute-start.1
  15.8 9.7 collective-permute-start.25
  54.8 15.4 %scatter.189 = f32[3,2,1,4,8,8,8]{6,5,4,3,1,0,2:T(8,128)S(1)} dynamic-update-slice(f32[3,2,1,4,8,8,8]{6,5,4,3,1,0,2:T(8,128)S(1)} %scatter.186, f32[3,2,1,4,8,8,1]{6,5,4,3,1,0,2:T(8,128)S(1)} %copy.186, s32[]{:T(128)} %constant.1319.clone.1, s32[]{:T(128)} %constant.1319.clone.1, s32[]{:T(128)} %constant.1319.clone.1, s32[]{:T(128)} %constant.1319.clone.1, s32[]{:T(128)} %constant.1319.clone.1, ...) | dynamic-update-slice | bytes 12292 | tf_op jit(solution)/shard_map/scatter | solution.py:64
  81.7 12.9 collective-permute-start.7
  114.6 4.7 collective-permute-done.11
  127.6 15.4 %scatter.199 = f32[3,2,1,4,8,8,8]{6,5,4,3,1,0,2:T(8,128)S(1)} dynamic-update-slice(f32[3,2,1,4,8,8,8]{6,5,4,3,1,0,2:T(8,128)S(1)} %scatter.196, f32[3,2,1,4,8,8,1]{6,5,4,3,1,0,2:T(8,128)S(1)} %copy.203, s32[]{:T(128)} %constant.1319.clone.1, s32[]{:T(128)} %constant.1319.clone.1, s32[]{:T(128)} %constant.1319.clone.1, s32[]{:T(128)} %constant.1319.clone.1, s32[]{:T(128)} %constant.1319.clone.1, ...) | dynamic-update-slice | bytes 12292 | tf_op jit(solution)/shard_map/scatter | solution.py:64
  152.5 12.7 collective-permute-start.13
  165.2 4.8 collective-permute-start.28
  199.0 15.4 %scatter.209 = f32[3,2,1,4,8,8,8]{6,5,4,3,1,0,2:T(8,128)S(1)} dynamic-update-slice(f32[3,2,1,4,8,8,8]{6,5,4,3,1,0,2:T(8,128)S(1)} %scatter.206, f32[3,2,1,4,8,8,1]{6,5,4,3,1,0,2:T(8,128)S(1)} %copy.220, s32[]{:T(128)} %constant.1319.clone.1, s32[]{:T(128)} %constant.1319.clone.1, s32[]{:T(128)} %constant.1319.clone.1, s32[]{:T(128)} %constant.1319.clone.1, s32[]{:T(128)} %constant.1319.clone.1, ...) | dynamic-update-slice | bytes 12292 | tf_op jit(solution)/shard_map/scatter | solution.py:64
  219.2 12.8 collective-permute-start.19
  252.8 4.8 scatter.219
  263.0 11.8 collective-permute-start.31
  299.1 63.1 %psum.85 = f32[]{:T(128)} all-reduce(f32[]{:T(128)} %get-tuple-element.810), channel_id=1, replica_groups=mesh['gx'=16,'gy'=4,'gz'=8] {'gy','gz'}, use_global_device_ids=true, to_apply=%region_4.17 | all-reduce | flops 1 | bytes 8 | tf_op jit(solution)/shard_map/psum | solution.py:185
  362.2 67.4 %psum.86 = f32[]{:T(128)} all-reduce(f32[]{:T(128)} %psum.85), channel_id=1, replica_groups=mesh['gx'=16,'gy'=4,'gz'=8] {'gx'}, use_global_device_ids=true, to_apply=%region_5.18 | all-reduce | flops 1 | bytes 8 | tf_op jit(solution)/shard_map/psum | solution.py:185
  429.6 93.5 %psum.84 = f32[]{:T(128)} all-reduce(f32[]{:T(128)} %get-tuple-element.811), channel_id=1, replica_groups=mesh['gx'=16,'gy'=4,'gz'=8] {'gx','gy','gz'}, use_global_device_ids=true, to_apply=%region_2.15 | all-reduce | flops 1 | bytes 8 | tf_op jit(solution)/shard_map/psum | solution.py:166
  525.2 94.4 %psum.87 = f32[]{:T(128)} all-reduce(f32[]{:T(128)} %get-tuple-element.860), channel_id=1, replica_groups=mesh['gx'=16,'gy'=4,'gz'=8] {'gx','gy','gz'}, use_global_device_ids=true, to_apply=%region_7.20 | all-reduce | flops 1 | bytes 8 | tf_op jit(solution)/shard_map/psum | solution.py:166
  655.9 61.5 %psum.88 = f32[]{:T(128)} all-reduce(f32[]{:T(128)} %fusion.31), channel_id=1, replica_groups=mesh['gx'=16,'gy'=4,'gz'=8] {'gy','gz'}, use_global_device_ids=true, to_apply=%region_9.22 | all-reduce | flops 1 | bytes 8 | tf_op jit(solution)/shard_map/psum | solution.py:185
  717.4 64.6 %psum.89 = f32[]{:T(128)} all-reduce(f32[]{:T(128)} %psum.88), channel_id=1, replica_groups=mesh['gx'=16,'gy'=4,'gz'=8] {'gx'}, use_global_device_ids=true, to_apply=%region_10.23 | all-reduce | flops 1 | bytes 8 | tf_op jit(solution)/shard_map/psum | solution.py:185
  784.7 93.5 %psum.90 = f32[]{:T(128)} all-reduce(f32[]{:T(128)} %get-tuple-element.857), channel_id=1, replica_groups=mesh['gx'=16,'gy'=4,'gz'=8] {'gx','gy','gz'}, use_global_device_ids=true, to_apply=%region_12.25 | all-reduce | flops 1 | bytes 8 | tf_op jit(solution)/shard_map/psum | solution.py:166
  913.2 62.4 %psum.91 = f32[]{:T(128)} all-reduce(f32[]{:T(128)} %fusion.33), channel_id=1, replica_groups=mesh['gx'=16,'gy'=4,'gz'=8] {'gy','gz'}, use_global_device_ids=true, to_apply=%region_14.27 | all-reduce | flops 1 | bytes 8 | tf_op jit(solution)/shard_map/psum | solution.py:185
  975.5 63.9 %psum.92 = f32[]{:T(128)} all-reduce(f32[]{:T(128)} %psum.91), channel_id=1, replica_groups=mesh['gx'=16,'gy'=4,'gz'=8] {'gx'}, use_global_device_ids=true, to_apply=%region_15.28 | all-reduce | flops 1 | bytes 8 | tf_op jit(solution)/shard_map/psum | solution.py:185
  1042.2 93.8 %psum.93 = f32[]{:T(128)} all-reduce(f32[]{:T(128)} %get-tuple-element.854), channel_id=1, replica_groups=mesh['gx'=16,'gy'=4,'gz'=8] {'gx','gy','gz'}, use_global_device_ids=true, to_apply=%region_17.30 | all-reduce | flops 1 | bytes 8 | tf_op jit(solution)/shard_map/psum | solution.py:166
  1171.6 62.4 %psum.94 = f32[]{:T(128)} all-reduce(f32[]{:T(128)} %fusion.35), channel_id=1, replica_groups=mesh['gx'=16,'gy'=4,'gz'=8] {'gy','gz'}, use_global_device_ids=true, to_apply=%region_19.32 | all-reduce | flops 1 | bytes 8 | tf_op jit(solution)/shard_map/psum | solution.py:185
  1235.0 63.1 %psum.95 = f32[]{:T(128)} all-reduce(f32[]{:T(128)} %psum.94), channel_id=1, replica_groups=mesh['gx'=16,'gy'=4,'gz'=8] {'gx'}, use_global_device_ids=true, to_apply=%region_20.33 | all-reduce | flops 1 | bytes 8 | tf_op jit(solution)/shard_map/psum | solution.py:185
  (576 shorter events, 278.5 us)
Async XLA Ops:
  2.1 27.2 %collective-permute-start = (f32[1,768]{1,0:T(1,128)S(1)}, f32[1,768]{1,0:T(1,128)S(1)}, u32[]{:S(2)}, u32[]{:S(2)}) collective-permute-start(f32[1,768]{1,0:T(1,128)S(1)} %get-tuple-element.943), channel_id=1, source_target_pairs={{0,32},{32,64},{64,96},{96,128},{128,160},{160,192},{192,224},{224... | collective-permute-start | bytes 9224 | tf_op jit(solution)/shard_map/ppermute | solution.py:20
  6.6 22.7 %collective-permute-start.1 = (f32[1,768]{1,0:T(1,128)S(1)}, f32[1,768]{1,0:T(1,128)S(1)}, u32[]{:S(2)}, u32[]{:S(2)}) collective-permute-start(f32[1,768]{1,0:T(1,128)S(1)} %get-tuple-element.944), channel_id=1, source_target_pairs={{32,0},{64,32},{96,64},{128,96},{160,128},{192,160},{224,192},{256... | collective-permute-start | bytes 9224 | tf_op jit(solution)/shard_map/ppermute | solution.py:23
  13.9 12.1 collective-permute-start.24
  15.8 10.5 collective-permute-start.25
  26.7 8.7 collective-permute-start.26
  28.1 7.3 collective-permute-start.27
  30.0 5.5 collective-permute-start.2
  79.4 15.9 %collective-permute-start.6 = (f32[1,768]{1,0:T(1,128)S(1)}, f32[1,768]{1,0:T(1,128)S(1)}, u32[]{:S(2)}, u32[]{:S(2)}) collective-permute-start(f32[1,768]{1,0:T(1,128)S(1)} %get-tuple-element.935), channel_id=1, source_target_pairs={{0,32},{32,64},{64,96},{96,128},{128,160},{160,192},{192,224},{224... | collective-permute-start | bytes 9224 | tf_op jit(solution)/shard_map/ppermute | solution.py:20
  81.7 13.7 %collective-permute-start.7 = (f32[1,768]{1,0:T(1,128)S(1)}, f32[1,768]{1,0:T(1,128)S(1)}, u32[]{:S(2)}, u32[]{:S(2)}) collective-permute-start(f32[1,768]{1,0:T(1,128)S(1)} %get-tuple-element.936), channel_id=1, source_target_pairs={{32,0},{64,32},{96,64},{128,96},{160,128},{192,160},{224,192},{256... | collective-permute-start | bytes 9224 | tf_op jit(solution)/shard_map/ppermute | solution.py:23
  113.2 6.2 collective-permute-start.11
  150.5 20.8 %collective-permute-start.12 = (f32[1,768]{1,0:T(1,128)S(1)}, f32[1,768]{1,0:T(1,128)S(1)}, u32[]{:S(2)}, u32[]{:S(2)}) collective-permute-start(f32[1,768]{1,0:T(1,128)S(1)} %get-tuple-element.927), channel_id=1, source_target_pairs={{0,32},{32,64},{64,96},{96,128},{128,160},{160,192},{192,224},{224... | collective-permute-start | bytes 9224 | tf_op jit(solution)/shard_map/ppermute | solution.py:20
  152.5 18.9 %collective-permute-start.13 = (f32[1,768]{1,0:T(1,128)S(1)}, f32[1,768]{1,0:T(1,128)S(1)}, u32[]{:S(2)}, u32[]{:S(2)}) collective-permute-start(f32[1,768]{1,0:T(1,128)S(1)} %get-tuple-element.928), channel_id=1, source_target_pairs={{32,0},{64,32},{96,64},{128,96},{160,128},{192,160},{224,192},{256... | collective-permute-start | bytes 9224 | tf_op jit(solution)/shard_map/ppermute | solution.py:23
  165.2 11.8 collective-permute-start.28
  170.1 6.9 collective-permute-start.29
  185.2 5.6 collective-permute-start.16
  217.2 14.7 %collective-permute-start.18 = (f32[1,256]{1,0:T(1,128)S(1)}, f32[1,256]{1,0:T(1,128)S(1)}, u32[]{:S(2)}, u32[]{:S(2)}) collective-permute-start(f32[1,256]{1,0:T(1,128)S(1)} %get-tuple-element.989), channel_id=1, source_target_pairs={{0,32},{32,64},{64,96},{96,128},{128,160},{160,192},{192,224},{224... | collective-permute-start | bytes 3080 | tf_op jit(solution)/shard_map/ppermute | solution.py:20
  219.2 13.6 %collective-permute-start.19 = (f32[1,256]{1,0:T(1,128)S(1)}, f32[1,256]{1,0:T(1,128)S(1)}, u32[]{:S(2)}, u32[]{:S(2)}) collective-permute-start(f32[1,256]{1,0:T(1,128)S(1)} %get-tuple-element.990), channel_id=1, source_target_pairs={{32,0},{64,32},{96,64},{128,96},{160,128},{192,160},{224,192},{256... | collective-permute-start | bytes 3080 | tf_op jit(solution)/shard_map/ppermute | solution.py:23
  240.3 11.0 collective-permute-start.22
  243.9 7.4 collective-permute-start.23
  261.1 13.8 %collective-permute-start.30 = (f32[1,256]{1,0:T(1,128)S(1)}, f32[1,256]{1,0:T(1,128)S(1)}, u32[]{:S(2)}, u32[]{:S(2)}) collective-permute-start(f32[1,256]{1,0:T(1,128)S(1)} %get-tuple-element.983), channel_id=1, source_target_pairs={{0,32},{32,64},{64,96},{96,128},{128,160},{160,192},{192,224},{224... | collective-permute-start | bytes 3080 | tf_op jit(solution)/shard_map/ppermute | solution.py:20
  263.0 12.7 collective-permute-start.31
  283.2 5.6 collective-permute-start.34
  883.0 6.2 collective-permute-start.42
  1140.7 6.2 collective-permute-start.48
  (38 other events, 272.0 us)
